TPU v7x, 32 devices: a whole 2x2x4 slice. The times are simulated.
32 devices in a mesh: ia: 4 (over x, core), ja: 2 (over y), ka: 4 (over z).
Axes of the slice: x: 2, y: 2, z: 4, core: 2. Of those that a mesh axis runs over, the one named last changes fastest.
Arguments:
- tensor: float32 [128, 256, 512], P('ia', 'ja', 'ka'), may hold values from -200 to 200
- factor_b: float32 [256, 4, 96], P(('ja', 'ka')), may hold values from -4 to 4
- factor_c: float32 [512, 4, 96], P(('ka', 'ja')), may hold values from -4 to 4
Outputs:
- factor_a: float32 [128, 4, 96], P(('ia', 'ja', 'ka'))
- weights: float32 [4, 96], replicated
All inputs are finite; a program needn't handle non-finite values.
Results may differ from a plain program's by a relative error of at most 0.0003.
Values sent between devices are 32-bit elements; how exact they have to be, the bound alone decides.
A program may use at most 64 MiB of HBM per device.

v0:
```python
import jax
import jax.numpy as jnp
from jax import lax
from jax.sharding import PartitionSpec as P

highest = lax.Precision.HIGHEST


def gram_of(rows):
    return jnp.einsum(
        "jsr,jsq->srq", rows, rows, precision=highest, preferred_element_type=jnp.float32
    )


def solve_normal(rows, gram_b, gram_c):
    columns = []
    for member in range(rows.shape[1]):
        normal_mat = gram_b[member] * gram_c[member]
        factor_l = jnp.linalg.cholesky(normal_mat)
        right_side = rows[:, member, :].T
        lower_sol = lax.linalg.triangular_solve(factor_l, right_side, left_side=True, lower=True)
        upper_sol = lax.linalg.triangular_solve(
            factor_l, lower_sol, left_side=True, lower=True, transpose_a=True
        )
        columns.append(upper_sol.T)
    return jnp.stack(columns, axis=1)


def shards(tensor, factor_b, factor_c):
    rows_i, rows_j, rows_k = tensor.shape
    starts, col_count = (factor_b.shape[1], factor_b.shape[2])
    width = starts * col_count
    c_block = lax.all_gather(factor_c, "ja", axis=0, tiled=True)
    partial_value = jnp.dot(
        tensor.reshape(rows_i * rows_j, rows_k),
        c_block.reshape(rows_k, width),
        precision=highest,
        preferred_element_type=jnp.float32,
    ).reshape(rows_i, rows_j, width)
    piece = lax.all_gather(factor_b, "ka", axis=0, tiled=True)
    gram_sum = jnp.zeros((starts, col_count, col_count), jnp.float32)
    count = piece.shape[0]
    flat_rows = piece.reshape(count, width)
    mttkrp = jnp.einsum(
        "ijr,jr->ir",
        partial_value,
        flat_rows,
        precision=highest,
        preferred_element_type=jnp.float32,
    )
    mttkrp, gram_rows = (mttkrp, gram_sum)
    gram_b, gram_c = lax.psum((gram_of(factor_b), gram_of(factor_c)), ("ja", "ka"))
    owned = lax.psum_scatter(mttkrp, ("ja", "ka"), scatter_dimension=0, tiled=True)
    owned = owned.reshape(owned.shape[0], starts, col_count)
    factor_raw = solve_normal(owned, gram_b, gram_c)
    squares = jnp.sum(factor_raw * factor_raw, axis=0)
    total = lax.psum(squares, ("ia", "ja", "ka"))
    row_total = rows_i * lax.axis_size("ia")
    weights = jnp.sqrt(total / row_total + 1e-06)
    return (factor_raw / weights[None], weights)


def solution(mesh):
    in_specs = (P("ia", "ja", "ka"), P(("ja", "ka"), None, None), P(("ka", "ja"), None, None))
    out_specs = (P(("ia", "ja", "ka"), None, None), P())
    return jax.shard_map(shards, mesh=mesh, in_specs=in_specs, out_specs=out_specs, check_vma=False)
```

profile of v0, /device:TPU:0, one launch (start us, length us, event | category | flops | bytes accessed | tf_op | source)
XLA Modules:
  0.0 222.9 jit_solution(2822683292989447386)
XLA Ops:
  7.2 0.0 all-reduce.4.cloned.1.call-start
  7.2 2.3 %fusion = f32[4,96,96]{1,2,0:T(8,128)} fusion(f32[64,4,96]{2,1,0:T(4,128)} %param.10), kind=kOutput, calls=%fused_computation.4 | convolution fusion | flops 28311552 | bytes 245760 | tf_op jit(solution)/shard_map/jsr,jsq->srq/dot_general | solution.py:10
  9.5 2.1 fusion.2
  11.6 0.0 all-reduce.4.cloned.1.call-update
  11.6 7.4 %all_gather.6 = f32[128,4,96]{2,1,0:T(4,128)S(1)} all-gather(f32[64,4,96]{2,1,0:T(4,128)} %param.10), channel_id=1, replica_groups=mesh['ia'=4,'ja'=2,'ka'=4] {'ja'}, dimensions={0}, use_global_device_ids=true | all-gather | bytes 294912 | tf_op jit(solution)/shard_map/all_gather | solution.py:33
  19.1 15.1 %all_gather.7 = f32[128,4,96]{2,1,0:T(4,128)S(1)} all-gather(f32[32,4,96]{2,1,0:T(4,128)} %param.9), channel_id=1, replica_groups=mesh['ia'=4,'ja'=2,'ka'=4] {'ka'}, dimensions={0}, use_global_device_ids=true | all-gather | bytes 245760 | tf_op jit(solution)/shard_map/all_gather | solution.py:40
  34.1 0.1 copy.36
  34.3 7.1 %fusion.28 = f32[32,128,384]{2,1,0:T(8,128)} fusion(f32[32,128,128]{2,1,0:T(8,128)S(1)} %copy-done, f32[128,384,1]{0,1,2:T(8,128)S(1)} %bitcast.130), kind=kOutput, calls=%fused_computation.63 | convolution fusion | flops 2415919104 | bytes 8585216 | tf_op jit(solution)/shard_map/dot_general | solution.py:34
  41.3 6.7 %copy.46 = f32[32,128,384]{1,0,2:T(8,128)} copy(f32[32,128,384]{2,1,0:T(8,128)} %fusion.28) | data formatting | bytes 12582912 | tf_op jit(solution)/shard_map/dot_general | solution.py:34
  48.0 0.1 copy.38
  48.2 11.9 %fusion.29 = f32[384,1,32]{2,1,0:T(1,128)S(1)} fusion(f32[32,128,384]{1,0,2:T(8,128)} %copy.46, f32[128,384,1]{0,2,1:T(1,128)S(1)} %bitcast.124), kind=kOutput, calls=%fused_computation.64 | convolution fusion | flops 18874368 | bytes 6537216 | tf_op jit(solution)/shard_map/ijr,jr->ir/dot_general | solution.py:44
  60.0 0.6 dynamic-slice
  61.3 41.9 %all-reduce = f32[32,384]{0,1:T(8,128)S(1)} all-reduce(f32[32,384]{0,1:T(8,128)S(1)} %bitcast.125), channel_id=2, replica_groups=mesh['ia'=4,'ja'=2,'ka'=4] {'ja','ka'}, use_global_device_ids=true, to_apply=%region_4.0.clone | all-reduce | flops 12288 | bytes 98304
  103.2 0.1 constant_dynamic-slice_fusion
  103.3 0.0 all-reduce.4.cloned.1.call-done
  103.4 1.0 fusion.24
  104.4 0.1 copy.35
  104.4 0.1 copy.41
  104.5 0.1 copy.40
  104.6 0.1 copy.39
  104.7 1.0 fusion.15
  105.7 8.8 %cholesky.107 = f32[96,96]{1,0:T(8,128)S(1)} custom-call(f32[96,96]{1,0:T(8,128)S(1)} %get-tuple-element.14), custom_call_target="Cholesky" | custom-call | tf_op jit(solution)/shard_map/jit(cholesky)/cholesky | solution.py:19
  114.5 0.6 compare_reduce_fusion
  115.2 0.7 fusion.7
  115.9 7.4 %custom-call.21 = f32[1,96,96]{1,2,0:T(8,128)S(1)} custom-call(f32[1,96,96]{2,1,0:T(8,128)S(1)} %fusion.7), custom_call_target="InvertDiagBlocksLowerTriangular" | custom-call | tf_op jit(solution)/shard_map/triangular_solve/custom-call.2 | solution.py:22
  123.2 0.2 fusion.8
  123.4 0.2 convolution_bitcast_fusion
  123.6 8.8 %cholesky.96 = f32[96,96]{1,0:T(8,128)S(1)} custom-call(f32[96,96]{1,0:T(8,128)S(1)} %get-tuple-element.15), custom_call_target="Cholesky" | custom-call | tf_op jit(solution)/shard_map/jit(cholesky)/cholesky | solution.py:19
  132.5 0.6 compare_reduce_fusion.1
  133.1 0.7 fusion.6
  133.8 7.4 %custom-call.19 = f32[1,96,96]{1,2,0:T(8,128)S(1)} custom-call(f32[1,96,96]{2,1,0:T(8,128)S(1)} %fusion.6), custom_call_target="InvertDiagBlocksLowerTriangular" | custom-call | tf_op jit(solution)/shard_map/triangular_solve/custom-call.2 | solution.py:22
  141.1 0.2 fusion.9
  141.3 0.2 convolution_bitcast_fusion.1
  141.5 8.8 %cholesky.85 = f32[96,96]{1,0:T(8,128)S(1)} custom-call(f32[96,96]{1,0:T(8,128)S(1)} %get-tuple-element.16), custom_call_target="Cholesky" | custom-call | tf_op jit(solution)/shard_map/jit(cholesky)/cholesky | solution.py:19
  150.4 0.6 compare_reduce_fusion.2
  151.0 0.7 fusion.5
  151.7 7.4 %custom-call.17 = f32[1,96,96]{1,2,0:T(8,128)S(1)} custom-call(f32[1,96,96]{2,1,0:T(8,128)S(1)} %fusion.5), custom_call_target="InvertDiagBlocksLowerTriangular" | custom-call | tf_op jit(solution)/shard_map/triangular_solve/custom-call.2 | solution.py:22
  159.1 0.2 fusion.10
  159.3 0.2 convolution_bitcast_fusion.2
  159.5 9.0 %cholesky.74 = f32[96,96]{1,0:T(8,128)S(1)} custom-call(f32[96,96]{1,0:T(8,128)S(1)} %get-tuple-element.13), custom_call_target="Cholesky" | custom-call | tf_op jit(solution)/shard_map/jit(cholesky)/cholesky | solution.py:19
  168.5 0.6 compare_reduce_fusion.3
  169.2 0.7 fusion.4
  169.8 7.4 %custom-call.15 = f32[1,96,96]{1,2,0:T(8,128)S(1)} custom-call(f32[1,96,96]{2,1,0:T(8,128)S(1)} %fusion.4), custom_call_target="InvertDiagBlocksLowerTriangular" | custom-call | tf_op jit(solution)/shard_map/triangular_solve/custom-call.2 | solution.py:22
  177.2 0.2 fusion.11
  177.4 0.2 convolution_bitcast_fusion.3
  177.6 0.1 multiply_reduce_fusion
  177.6 37.8 %psum.23 = f32[4,96]{1,0:T(4,128)S(1)} all-reduce(f32[4,96]{1,0:T(4,128)S(1)} %multiply_reduce_fusion), channel_id=1, replica_groups=mesh['ia'=4,'ja'=2,'ka'=4] {'ia','ja','ka'}, use_global_device_ids=true, to_apply=%region_6.10 | all-reduce | flops 384 | bytes 3072 | tf_op jit(solution)/shard_map/psum | solution.py:57
  215.5 0.6 copy.42
  (12 shorter events, 0.2 us)
Async XLA Ops:
  7.2 27.1 %copy-start = (f32[32,128,128]{2,1,0:T(8,128)S(1)}, f32[32,128,128]{2,1,0:T(8,128)}, u32[]{:S(2)}) copy-start(f32[32,128,128]{2,1,0:T(8,128)} %param.8) | copy-start | bytes 6291460
  7.2 96.2 %all-reduce.4.cloned.1.call-start = ((), (), s32[]{:S(2)}) async-start(), calls=%async_computation | async-start | bytes 786432 | tf_op jit(solution)/shard_map/psum | solution.py:52
  48.0 12.0 %copy-start.2 = (u32[32]{0:T(128)S(1)}, u32[32]{0:T(128)}, u32[]{:S(2)}) copy-start(u32[32]{0:T(128)} %constant.41) | copy-start | bytes 388
  215.4 0.6 copy-start.1
Sparse Core Ops, SparseCore 0:
  11.8 75.5 all-reduce.3
where the time goes:
time: 223 us
  blocking collectives  102 us (46%)
  other arithmetic  72.3 us (32%)
  matrix products  24.9 us (11%)
  between operations  14.9 us (7%)
  local copies, waits for them, and re-layouts  8.59 us (4%)
    unnamed x1, blocking collectives  41.9 us
    another operation x12, other arithmetic, solve_normal(): factor_l = jnp.linalg.cholesky(normal_mat)  38.1 us
    psum x1, blocking collectives, shards(): total = lax.psum(squares, ('ia', 'ja', 'ka'))  37.8 us
    another operation x8, other arithmetic, solve_normal(): lax.linalg.triangular_solve(factor_l, lower_sol, left_side=True, lower=Tr...  32 us
    all_gather x1, blocking collectives, shards(): piece = lax.all_gather(factor_b, 'ka', axis=0, tiled=True)  15.1 us
    dot_general x1, matrix products, shards(): jnp.einsum('ijr,jr->ir', partial_value, flat_rows, precision=highest, pre...  11.9 us
    all_gather x1, blocking collectives, shards(): c_block = lax.all_gather(factor_c, 'ja', axis=0, tiled=True)  7.42 us
    dot_general x1, matrix products, shards(): jnp.dot(tensor.reshape(rows_i * rows_j, rows_k), c_block.reshape(rows_k,...  7.07 us
  transfers between devices with their start and end apart: 1, of which 0 were waited for; matrix products, arithmetic and copies ran while one was open for 12% of the time, Pallas kernels for 0%

commit v1 on v0

--- a/solution.py
+++ b/solution.py
@@ -54,7 +54,7 @@
     owned = owned.reshape(owned.shape[0], starts, col_count)
     factor_raw = solve_normal(owned, gram_b, gram_c)
     squares = jnp.sum(factor_raw * factor_raw, axis=0)
-    total = lax.psum(squares, ("ia", "ja", "ka"))
+    total = lax.psum(lax.psum(squares, ("ja", "ka")), "ia")
     row_total = rows_i * lax.axis_size("ia")
     weights = jnp.sqrt(total / row_total + 1e-06)
     return (factor_raw / weights[None], weights)

time: 223 us -> 208 us (0.933)
  blocking collectives: 102 us -> 87.3 us
    psum x1 -> x2, blocking collectives: 37.8 us -> 22.9 us  [shards(): total = lax.psum(lax.psum(squares, ('ja', 'ka')), 'ia')]
  transfers between devices with their start and end apart: 1 -> 1, of which waited for: 0 -> 0; matrix products, arithmetic and copies ran while one was open for 12% -> 13% of each run, Pallas kernels for 0% -> 0%
where the time goes in v1:
time: 208 us
  blocking collectives  87.3 us (42%)
  other arithmetic  72.3 us (35%)
  matrix products  24.9 us (12%)
  between operations  14.9 us (7%)
  local copies, waits for them, and re-layouts  8.6 us (4%)
    unnamed x1, blocking collectives  41.9 us
    another operation x12, other arithmetic, solve_normal(): factor_l = jnp.linalg.cholesky(normal_mat)  38.1 us
    another operation x8, other arithmetic, solve_normal(): lax.linalg.triangular_solve(factor_l, lower_sol, left_side=True, lower=Tr...  32 us
    psum x2, blocking collectives, shards(): total = lax.psum(lax.psum(squares, ('ja', 'ka')), 'ia')  22.9 us
    all_gather x1, blocking collectives, shards(): piece = lax.all_gather(factor_b, 'ka', axis=0, tiled=True)  15.1 us
    dot_general x1, matrix products, shards(): jnp.einsum('ijr,jr->ir', partial_value, flat_rows, precision=highest, pre...  11.9 us
    all_gather x1, blocking collectives, shards(): c_block = lax.all_gather(factor_c, 'ja', axis=0, tiled=True)  7.42 us
    dot_general x1, matrix products, shards(): jnp.dot(tensor.reshape(rows_i * rows_j, rows_k), c_block.reshape(rows_k,...  7.07 us
  transfers between devices with their start and end apart: 1, of which 0 were waited for; matrix products, arithmetic and copies ran while one was open for 13% of the time, Pallas kernels for 0%

profile of v1, /device:TPU:0, one launch (start us, length us, event | category | flops | bytes accessed | tf_op | source)
XLA Modules:
  0.0 208.0 jit_solution(1358652794117732678)
XLA Ops:
  7.2 0.0 all-reduce.4.cloned.1.call-start
  7.2 2.3 %fusion = f32[4,96,96]{1,2,0:T(8,128)} fusion(f32[64,4,96]{2,1,0:T(4,128)} %param.10), kind=kOutput, calls=%fused_computation.4 | convolution fusion | flops 28311552 | bytes 245760 | tf_op jit(solution)/shard_map/jsr,jsq->srq/dot_general | solution.py:10
  9.5 2.1 %fusion.2 = f32[4,96,96]{1,2,0:T(8,128)} fusion(f32[32,4,96]{2,1,0:T(4,128)} %param.9), kind=kOutput, calls=%fused_computation.6 | convolution fusion | flops 14155776 | bytes 196608 | tf_op jit(solution)/shard_map/jsr,jsq->srq/dot_general | solution.py:10
  11.6 7.4 %all_gather.6 = f32[128,4,96]{2,1,0:T(4,128)S(1)} all-gather(f32[64,4,96]{2,1,0:T(4,128)} %param.10), channel_id=1, replica_groups=mesh['ia'=4,'ja'=2,'ka'=4] {'ja'}, dimensions={0}, use_global_device_ids=true | all-gather | bytes 294912 | tf_op jit(solution)/shard_map/all_gather | solution.py:33
  19.1 15.1 %all_gather.7 = f32[128,4,96]{2,1,0:T(4,128)S(1)} all-gather(f32[32,4,96]{2,1,0:T(4,128)} %param.9), channel_id=1, replica_groups=mesh['ia'=4,'ja'=2,'ka'=4] {'ka'}, dimensions={0}, use_global_device_ids=true | all-gather | bytes 245760 | tf_op jit(solution)/shard_map/all_gather | solution.py:40
  34.1 0.1 copy.36
  34.3 7.1 %fusion.28 = f32[32,128,384]{2,1,0:T(8,128)} fusion(f32[32,128,128]{2,1,0:T(8,128)S(1)} %copy-done, f32[128,384,1]{0,1,2:T(8,128)S(1)} %bitcast.130), kind=kOutput, calls=%fused_computation.63 | convolution fusion | flops 2415919104 | bytes 8585216 | tf_op jit(solution)/shard_map/dot_general | solution.py:34
  41.3 6.7 %copy.46 = f32[32,128,384]{1,0,2:T(8,128)} copy(f32[32,128,384]{2,1,0:T(8,128)} %fusion.28) | data formatting | bytes 12582912 | tf_op jit(solution)/shard_map/dot_general | solution.py:34
  48.0 0.1 copy.38
  48.2 11.9 %fusion.29 = f32[384,1,32]{2,1,0:T(1,128)S(1)} fusion(f32[32,128,384]{1,0,2:T(8,128)} %copy.46, f32[128,384,1]{0,2,1:T(1,128)S(1)} %bitcast.124), kind=kOutput, calls=%fused_computation.64 | convolution fusion | flops 18874368 | bytes 6537216 | tf_op jit(solution)/shard_map/ijr,jr->ir/dot_general | solution.py:44
  60.0 0.6 dynamic-slice
  61.3 41.9 %all-reduce = f32[32,384]{0,1:T(8,128)S(1)} all-reduce(f32[32,384]{0,1:T(8,128)S(1)} %bitcast.125), channel_id=2, replica_groups=mesh['ia'=4,'ja'=2,'ka'=4] {'ja','ka'}, use_global_device_ids=true, to_apply=%region_4.0.clone | all-reduce | flops 12288 | bytes 98304
  103.2 0.1 constant_dynamic-slice_fusion
  103.3 0.0 all-reduce.4.cloned.1.call-done
  103.4 1.0 fusion.24
  104.4 0.1 copy.35
  104.4 0.1 copy.41
  104.5 0.1 copy.40
  104.6 0.1 copy.39
  104.7 1.0 fusion.15
  105.7 8.8 %cholesky.107 = f32[96,96]{1,0:T(8,128)S(1)} custom-call(f32[96,96]{1,0:T(8,128)S(1)} %get-tuple-element.14), custom_call_target="Cholesky" | custom-call | tf_op jit(solution)/shard_map/jit(cholesky)/cholesky | solution.py:19
  114.5 0.6 compare_reduce_fusion
  115.2 0.7 fusion.7
  115.9 7.4 %custom-call.21 = f32[1,96,96]{1,2,0:T(8,128)S(1)} custom-call(f32[1,96,96]{2,1,0:T(8,128)S(1)} %fusion.7), custom_call_target="InvertDiagBlocksLowerTriangular" | custom-call | tf_op jit(solution)/shard_map/triangular_solve/custom-call.2 | solution.py:22
  123.2 0.2 fusion.8
  123.4 0.2 convolution_bitcast_fusion
  123.6 8.8 %cholesky.96 = f32[96,96]{1,0:T(8,128)S(1)} custom-call(f32[96,96]{1,0:T(8,128)S(1)} %get-tuple-element.15), custom_call_target="Cholesky" | custom-call | tf_op jit(solution)/shard_map/jit(cholesky)/cholesky | solution.py:19
  132.5 0.6 compare_reduce_fusion.1
  133.1 0.7 fusion.6
  133.8 7.4 %custom-call.19 = f32[1,96,96]{1,2,0:T(8,128)S(1)} custom-call(f32[1,96,96]{2,1,0:T(8,128)S(1)} %fusion.6), custom_call_target="InvertDiagBlocksLowerTriangular" | custom-call | tf_op jit(solution)/shard_map/triangular_solve/custom-call.2 | solution.py:22
  141.1 0.2 fusion.9
  141.3 0.2 convolution_bitcast_fusion.1
  141.5 8.8 %cholesky.85 = f32[96,96]{1,0:T(8,128)S(1)} custom-call(f32[96,96]{1,0:T(8,128)S(1)} %get-tuple-element.16), custom_call_target="Cholesky" | custom-call | tf_op jit(solution)/shard_map/jit(cholesky)/cholesky | solution.py:19
  150.4 0.6 compare_reduce_fusion.2
  151.0 0.7 fusion.5
  151.7 7.4 %custom-call.17 = f32[1,96,96]{1,2,0:T(8,128)S(1)} custom-call(f32[1,96,96]{2,1,0:T(8,128)S(1)} %fusion.5), custom_call_target="InvertDiagBlocksLowerTriangular" | custom-call | tf_op jit(solution)/shard_map/triangular_solve/custom-call.2 | solution.py:22
  159.1 0.2 fusion.10
  159.3 0.2 convolution_bitcast_fusion.2
  159.5 9.0 %cholesky.74 = f32[96,96]{1,0:T(8,128)S(1)} custom-call(f32[96,96]{1,0:T(8,128)S(1)} %get-tuple-element.13), custom_call_target="Cholesky" | custom-call | tf_op jit(solution)/shard_map/jit(cholesky)/cholesky | solution.py:19
  168.5 0.6 compare_reduce_fusion.3
  169.2 0.7 fusion.4
  169.8 7.4 %custom-call.15 = f32[1,96,96]{1,2,0:T(8,128)S(1)} custom-call(f32[1,96,96]{2,1,0:T(8,128)S(1)} %fusion.4), custom_call_target="InvertDiagBlocksLowerTriangular" | custom-call | tf_op jit(solution)/shard_map/triangular_solve/custom-call.2 | solution.py:22
  177.2 0.2 fusion.11
  177.4 0.2 convolution_bitcast_fusion.3
  177.6 0.1 multiply_reduce_fusion
  177.6 17.2 %psum.30 = f32[4,96]{1,0:T(4,128)S(1)} all-reduce(f32[4,96]{1,0:T(4,128)S(1)} %multiply_reduce_fusion), channel_id=1, replica_groups=mesh['ia'=4,'ja'=2,'ka'=4] {'ja','ka'}, use_global_device_ids=true, to_apply=%region_6.10 | all-reduce | flops 384 | bytes 3072 | tf_op jit(solution)/shard_map/psum | solution.py:57
  194.9 5.6 %psum.31 = f32[4,96]{1,0:T(4,128)S(1)} all-reduce(f32[4,96]{1,0:T(4,128)S(1)} %psum.30), channel_id=1, replica_groups=mesh['ia'=4,'ja'=2,'ka'=4] {'ia'}, use_global_device_ids=true, to_apply=%region_7.11 | all-reduce | flops 384 | bytes 3072 | tf_op jit(solution)/shard_map/psum | solution.py:57
  200.5 0.6 copy.42
  (13 shorter events, 0.2 us)
Async XLA Ops:
  7.2 27.1 %copy-start = (f32[32,128,128]{2,1,0:T(8,128)S(1)}, f32[32,128,128]{2,1,0:T(8,128)}, u32[]{:S(2)}) copy-start(f32[32,128,128]{2,1,0:T(8,128)} %param.8) | copy-start | bytes 6291460
  7.2 96.2 %all-reduce.4.cloned.1.call-start = ((), (), s32[]{:S(2)}) async-start(), calls=%async_computation | async-start | bytes 786432 | tf_op jit(solution)/shard_map/psum | solution.py:52
  48.0 12.0 %copy-start.2 = (u32[32]{0:T(128)S(1)}, u32[32]{0:T(128)}, u32[]{:S(2)}) copy-start(u32[32]{0:T(128)} %constant.41) | copy-start | bytes 388
  200.5 0.6 copy-start.1
Sparse Core Ops, SparseCore 0:
  11.8 75.5 all-reduce.3
